TPU v7x, 32 devices: a whole 2x2x4 slice. The times are simulated.
32 devices in a mesh: tok: 8 (over z, x), head: 4 (over y, core).
Axes of the slice: x: 2, y: 2, z: 4, core: 2. Of those that a mesh axis runs over, the one named last changes fastest.
Arguments:
- queries: bfloat16 [2048, 8192], P(('tok', 'head')), may hold values from -6 to 6
- keys: bfloat16 [2048, 1024], P(('tok', 'head')), may hold values from -6 to 6
- values: bfloat16 [2048, 1024], P(('tok', 'head')), may hold values from -6 to 6
- doc_ids: int32 [2048], replicated, may hold values from 0 to 2, never falling along the last dimension, each value on 1 to 1792 neighbouring positions
Outputs:
- attention: bfloat16 [2048, 8192], P('tok', 'head')
Inputs may be any that keep to these rules, and one draw needn't show every extreme that they name: doc_ids never falls along the tokens; each document holds 1 to 1792 tokens and some document holds exactly 1792.
All inputs are finite; a program needn't handle non-finite values.
Results may differ from a plain program's by a relative error of at most 0.0038.
Values may be sent and summed in bfloat16 or wider, within the bound.
A program may use at most 64 MiB of HBM per device.

v0:
```python
import jax
import jax.numpy as jnp
from jax import lax
from jax.sharding import PartitionSpec as P

QH = 64
KVH = 8
HD = 128
REACH = 7


def from_behind(array, axis, by):
    length = lax.axis_size(axis)
    pairs = [(i, i + by) for i in range(length) if 0 <= i + by < length]
    return lax.ppermute(array, axis, pairs)


def body(queries, keys, values, doc_ids):
    local_queries, local_keys, local_values = (
        lax.all_to_all(queries, "head", split_axis=1, concat_axis=0, tiled=True),
        lax.all_to_all(keys, "head", split_axis=1, concat_axis=0, tiled=True),
        lax.all_to_all(values, "head", split_axis=1, concat_axis=0, tiled=True),
    )
    shard_rows = local_queries.shape[0]
    head_count = local_keys.shape[1] // HD
    groups = QH // KVH
    scaling = HD ** (-0.5)
    query_heads = local_queries.reshape(shard_rows, head_count, groups, HD)
    shard_index = lax.axis_index("tok")
    padded_ids = jnp.concatenate([jnp.full((REACH * shard_rows,), -1, jnp.int32), doc_ids], axis=0)
    own_ids = lax.dynamic_slice_in_dim(
        padded_ids, (shard_index + REACH) * shard_rows, shard_rows, 0
    )
    causal = jnp.arange(shard_rows)[None, :] <= jnp.arange(shard_rows)[:, None]

    def absorb(carry_state, key_pair, offset):
        key_ids = lax.dynamic_slice_in_dim(
            padded_ids, (shard_index + REACH - offset) * shard_rows, shard_rows, 0
        )
        visible = own_ids[:, None] == key_ids[None, :]
        if offset == 0:
            visible = visible & causal
        peak_now, weight_sum, numerator = carry_state
        key_block = key_pair[0].reshape(shard_rows, head_count, HD)
        value_block = key_pair[1].reshape(shard_rows, head_count, HD)
        scores = (
            jnp.einsum("qcgd,kcd->qcgk", query_heads, key_block, preferred_element_type=jnp.float32)
            * scaling
        )
        scores = jnp.where(visible[:, None, None, :], scores, -jnp.inf)
        peak_new = jnp.maximum(peak_now, jnp.max(scores, axis=-1))
        rescale = jnp.exp(peak_now - peak_new)
        weights = jnp.exp(scores - peak_new[..., None])
        weight_sum = weight_sum * rescale + jnp.sum(weights, axis=-1)
        rounded = weights.astype(jnp.bfloat16)
        numerator = numerator * rescale[..., None] + jnp.einsum(
            "qcgk,kcd->qcgd", rounded, value_block, preferred_element_type=jnp.float32
        )
        return (peak_new, weight_sum, numerator)

    start_state = (
        jnp.full((shard_rows, head_count, groups), -jnp.inf, jnp.float32),
        jnp.zeros((shard_rows, head_count, groups), jnp.float32),
        jnp.zeros((shard_rows, head_count, groups, HD), jnp.float32),
    )
    own_pair = jnp.stack([local_keys, local_values], axis=0)
    carry_state = absorb(start_state, own_pair, 0)
    window = own_pair[None]
    for section_level in range(REACH.bit_length()):
        extent = window.shape[0]
        arrived = from_behind(window, "tok", extent)
        for position in range(extent):
            offset = 2 * extent - 1 - position
            carry_state = absorb(carry_state, arrived[position], offset)
        window = jnp.concatenate([arrived, window], axis=0)
    peak_now, weight_sum, numerator = carry_state
    result = numerator / weight_sum[..., None]
    return result.reshape(shard_rows, head_count * groups * HD).astype(jnp.bfloat16)


def solution(mesh):
    return jax.shard_map(
        body,
        mesh=mesh,
        in_specs=(
            P(("tok", "head"), None),
            P(("tok", "head"), None),
            P(("tok", "head"), None),
            P(),
        ),
        out_specs=P("tok", "head"),
        check_vma=False,
    )
```

profile of v0, /device:TPU:25, one launch (start us, length us, event | category | flops | bytes accessed | tf_op | source)
XLA Modules:
  0.0 129.8 jit_solution(17575146356472023909)
XLA Ops:
  0.0 1.6 %copy.234 = bf16[8,4,8,256]{3,2,0,1:T(8,128)(2,1)} copy(bf16[8,4,8,256]{3,2,1,0:T(8,128)(2,1)} %bitcast.264) | data formatting | bytes 262144 | tf_op jit(solution)/shard_map/all_to_all | solution.py:21
  1.6 4.0 %all-to-all-start = ((bf16[64,4,256]{2,0,1:T(8,128)(2,1)}), bf16[64,4,256]{2,0,1:T(8,128)(2,1)S(1)}, u32[]{:S(2)}, u32[]{:S(2)}) async-start(bf16[64,4,256]{2,0,1:T(8,128)(2,1)} %bitcast.233), calls=%async_computation | async-start | bytes 262144 | tf_op jit(solution)/shard_map/all_to_all | solution.py:21
  5.6 1.5 %copy.233 = bf16[8,4,8,256]{3,2,0,1:T(8,128)(2,1)} copy(bf16[8,4,8,256]{3,2,1,0:T(8,128)(2,1)} %bitcast.265) | data formatting | bytes 262144 | tf_op jit(solution)/shard_map/all_to_all | solution.py:22
  7.1 2.0 %all-to-all-done = bf16[64,4,256]{2,0,1:T(8,128)(2,1)S(1)} async-done(((bf16[64,4,256]{2,0,1:T(8,128)(2,1)}), bf16[64,4,256]{2,0,1:T(8,128)(2,1)S(1)}, u32[]{:S(2)}, u32[]{:S(2)}) %all-to-all-start) | async-done | bytes 131104 | tf_op jit(solution)/shard_map/all_to_all | solution.py:21
  9.1 4.3 %all-to-all-start.2 = ((bf16[64,4,256]{2,0,1:T(8,128)(2,1)}), bf16[64,4,256]{2,0,1:T(8,128)(2,1)S(1)}, u32[]{:S(2)}, u32[]{:S(2)}) async-start(bf16[64,4,256]{2,0,1:T(8,128)(2,1)} %bitcast.232), calls=%async_computation.2 | async-start | bytes 262144 | tf_op jit(solution)/shard_map/all_to_all | solution.py:22
  13.4 2.3 %copy.232 = bf16[8,4,8,2048]{3,2,0,1:T(8,128)(2,1)} copy(bf16[8,4,8,2048]{3,2,1,0:T(8,128)(2,1)} %bitcast.247) | data formatting | bytes 2097152 | tf_op jit(solution)/shard_map/all_to_all | solution.py:20
  15.8 1.3 all-to-all-done.2
  17.0 4.5 %all-to-all-start.1 = ((bf16[64,4,2048]{2,0,1:T(8,128)(2,1)}), bf16[64,4,2048]{2,0,1:T(8,128)(2,1)S(1)}, u32[]{:S(2)}, u32[]{:S(2)}) async-start(bf16[64,4,2048]{2,0,1:T(8,128)(2,1)} %bitcast.231), calls=%async_computation.1 | async-start | bytes 2097152 | tf_op jit(solution)/shard_map/all_to_all | solution.py:20
  21.6 3.1 %collective-permute-start = (bf16[1,2,256,256]{3,2,1,0:T(8,128)(2,1)S(1)}, bf16[1,2,256,256]{3,2,1,0:T(8,128)(2,1)S(1)}, u32[]{:S(2)}, u32[]{:S(2)}) collective-permute-start(bf16[1,2,256,256]{3,2,1,0:T(8,128)(2,1)S(1)} %maximum_bitcast_fusion), channel_id=1, source_target_pairs={{0,4},{4,8},{8,12},{12,16},{16,20},{20,24},{24,28},{1,5},{5,9},{9,... | collective-permute-start | bytes 786440 | tf_op jit(solution)/shard_map/ppermute | solution.py:15
  24.8 1.0 broadcast_compare_fusion.6
  26.6 0.7 reshape_squeeze_stack.7
  27.3 4.9 %collective-permute-done = bf16[1,2,256,256]{3,2,1,0:T(8,128)(2,1)S(1)} collective-permute-done((bf16[1,2,256,256]{3,2,1,0:T(8,128)(2,1)S(1)}, bf16[1,2,256,256]{3,2,1,0:T(8,128)(2,1)S(1)}, u32[]{:S(2)}, u32[]{:S(2)}) %collective-permute-start) | collective-permute-done | bytes 262176 | tf_op jit(solution)/shard_map/ppermute | solution.py:15
  32.2 0.7 copy.112
  33.0 0.8 copy.109
  33.7 0.8 pad_maximum_fusion.1
  34.5 1.3 collective-permute-start.1
  36.1 1.8 %fusion.16 = (f32[256,2,8]{0,2,1:T(8,128)S(1)}, f32[2,256,256,8]{2,1,3,0:T(8,128)S(1)}) fusion(pred[256,256]{0,1:T(8,128)(4,1)S(1)} %get-tuple-element.50, bf16[256,2,8,128]{3,2,1,0:T(8,128)(2,1)S(1)} %bitcast.234, bf16[256,2,128,1]{2,1,0,3:T(2,128)(2,1)} %bitcast.258), kind=kOutput, calls=%fused_computation.32 | convolution fusion | flops 271577088 | bytes 5455872 | tf_op jit(solution)/shard_map/qcgd,kcd->qcgk/dot_general | solution.py:47
  37.9 3.7 %fusion.38 = f32[2,256,8,128]{1,3,2,0:T(8,128)} fusion(f32[2,256,256,8]{2,1,3,0:T(8,128)S(1)} %get-tuple-element.64, f32[256,2,8]{0,2,1:T(8,128)S(1)} %get-tuple-element.63, pred[256,256]{0,1:T(8,128)(4,1)S(1)} %get-tuple-element.50, bf16[256,2,128,1]{2,1,0,3:T(2,128)(2,1)} %bitcast.257), kind=kOutput, calls=%fused_computation.47 | convolution fusion | flops 272629760 | bytes 6504448 | tf_op jit(solution)/shard_map/qcgk,kcd->qcgd/dot_general | solution.py:56
  41.6 7.6 %collective-permute-done.1 = bf16[2,2,256,256]{3,2,1,0:T(8,128)(2,1)S(1)} collective-permute-done((bf16[2,2,256,256]{3,2,1,0:T(8,128)(2,1)}, bf16[2,2,256,256]{3,2,1,0:T(8,128)(2,1)S(1)}, u32[]{:S(2)}, u32[]{:S(2)}) %collective-permute-start.1) | collective-permute-done | bytes 524320 | tf_op jit(solution)/shard_map/ppermute | solution.py:15
  49.2 1.1 pad_maximum_fusion
  50.3 1.5 %collective-permute-start.2 = (bf16[4,2,256,256]{3,2,1,0:T(8,128)(2,1)}, bf16[4,2,256,256]{3,2,1,0:T(8,128)(2,1)S(1)}, u32[]{:S(2)}, u32[]{:S(2)}) collective-permute-start(bf16[4,2,256,256]{3,2,1,0:T(8,128)(2,1)} %pad_maximum_fusion), channel_id=1, source_target_pairs={{0,16},{4,20},{8,24},{12,28},{1,17},{5,21},{9,25},{13,29},{2,18},{... | collective-permute-start | bytes 3145736 | tf_op jit(solution)/shard_map/ppermute | solution.py:15
  51.8 3.5 %fusion.17 = (f32[256,2,8]{0,2,1:T(8,128)}, f32[2,256,256,8]{2,1,3,0:T(8,128)}) fusion(pred[256,256]{0,1:T(8,128)(4,1)S(1)} %get-tuple-element.43, bf16[256,2,128,1]{0,2,3,1:T(8,128)(2,1)S(1)} %bitcast.255, bf16[256,2,8,128]{3,2,1,0:T(8,128)(2,1)S(1)} %bitcast.235), kind=kOutput, calls=%fused_computation.33 | convolution fusion | flops 271577088 | bytes 5455872 | tf_op jit(solution)/shard_map/qcgd,kcd->qcgk/dot_general | solution.py:47
  55.3 0.7 fusion.120
  56.3 1.0 copy.114
  57.3 3.5 %fusion.18 = (f32[256,2,8]{0,2,1:T(8,128)}, f32[2,256,256,8]{2,1,3,0:T(8,128)}) fusion(pred[256,256]{0,1:T(8,128)(4,1)S(1)} %get-tuple-element.44, bf16[256,2,128,1]{0,2,3,1:T(8,128)(2,1)S(1)} %bitcast.262, bf16[256,2,8,128]{3,2,1,0:T(8,128)(2,1)S(1)} %bitcast.236), kind=kOutput, calls=%fused_computation.34 | convolution fusion | flops 271577088 | bytes 5455872 | tf_op jit(solution)/shard_map/qcgd,kcd->qcgk/dot_general | solution.py:47
  60.9 3.5 %fusion.19 = (f32[256,2,8]{0,2,1:T(8,128)}, f32[2,256,256,8]{2,1,3,0:T(8,128)}) fusion(pred[256,256]{0,1:T(8,128)(4,1)S(1)} %get-tuple-element.45, bf16[256,2,128,1]{0,2,3,1:T(8,128)(2,1)S(1)} %bitcast.261, bf16[256,2,8,128]{3,2,1,0:T(8,128)(2,1)S(1)} %bitcast.237), kind=kOutput, calls=%fused_computation.35 | convolution fusion | flops 271577088 | bytes 5455872 | tf_op jit(solution)/shard_map/qcgd,kcd->qcgk/dot_general | solution.py:47
  64.4 36.4 %collective-permute-done.2 = bf16[4,2,256,256]{3,2,1,0:T(8,128)(2,1)S(1)} collective-permute-done((bf16[4,2,256,256]{3,2,1,0:T(8,128)(2,1)}, bf16[4,2,256,256]{3,2,1,0:T(8,128)(2,1)S(1)}, u32[]{:S(2)}, u32[]{:S(2)}) %collective-permute-start.2) | collective-permute-done | bytes 1048608 | tf_op jit(solution)/shard_map/ppermute | solution.py:15
  100.7 0.8 fusion.119
  101.9 1.0 copy.132
  103.0 1.0 copy.127
  104.2 1.0 fusion.20
  105.2 1.0 fusion.21
  106.2 1.0 fusion.22
  107.2 1.0 fusion.23
  108.2 1.1 fusion.28
  109.4 2.0 %fusion.8 = (f32[256,2,8]{0,2,1:T(8,128)S(1)}, f32[256,2,8]{0,2,1:T(8,128)S(1)}) fusion(f32[2,256,256,8]{2,1,3,0:T(8,128)S(1)} %get-tuple-element.58, f32[256,2,8]{0,2,1:T(8,128)S(1)} %get-tuple-element.16, pred[256,256]{0,1:T(8,128)(4,1)S(1)} %get-tuple-element.46, f32[256,2,8]{0,2,1:T(8,128)S(1)} %get-tuple-element.15, ...), kind=kLoop, calls=%fused_computation.24 | loop fusion | flops 8380416 | bytes 8585216 | tf_op jit(solution)/shard_map/reduce_sum | solution.py:54
  111.4 1.1 fusion.30
  112.6 1.0 copy-done.4
  113.6 1.4 %fusion.32 = f32[2,128,256,8]{2,1,3,0:T(8,128)S(1)} fusion(bf16[256,2,128,1]{0,2,3,1:T(8,128)(2,1)S(1)} %bitcast.251, f32[2,256,256,8]{2,1,3,0:T(8,128)S(1)} %copy-done.4, f32[256,2,8]{0,2,1:T(8,128)S(1)} %get-tuple-element.17, pred[256,256]{0,1:T(8,128)(4,1)S(1)} %get-tuple-element.45), kind=kOutput, calls=%fused_computation.44 | convolution fusion | flops 272629760 | bytes 6504448 | tf_op jit(solution)/shard_map/qcgk,kcd->qcgd/dot_general | solution.py:56
  115.1 2.0 %fusion.4 = (f32[256,2,8]{0,2,1:T(8,128)S(1)}, f32[256,2,8]{0,2,1:T(8,128)S(1)}) fusion(f32[2,256,256,8]{2,1,3,0:T(8,128)S(1)} %copy-done.3, f32[256,2,8]{0,2,1:T(8,128)S(1)} %get-tuple-element.18, pred[256,256]{0,1:T(8,128)(4,1)S(1)} %get-tuple-element.44, f32[256,2,8]{0,2,1:T(8,128)S(1)} %get-tuple-element.17, f32[2,256,256,8]{2,1,3,0:T(8,128)S(1)} %copy-done.4, ...), kind=kLoop, calls=%fused_computation.20 | loop fusion | flops 8380416 | bytes 8585216 | tf_op jit(solution)/shard_map/reduce_sum | solution.py:54
  117.2 1.1 fusion.34
  118.3 1.1 copy-done.1
  119.4 2.0 %fusion = (f32[256,2,8]{0,2,1:T(8,128)S(1)}, f32[256,2,8]{0,2,1:T(8,128)S(1)}) fusion(f32[2,256,256,8]{2,1,3,0:T(8,128)S(1)} %copy-done.1, f32[256,2,8]{0,2,1:T(8,128)S(1)} %get-tuple-element.63, pred[256,256]{0,1:T(8,128)(4,1)S(1)} %get-tuple-element.50, f32[256,2,8]{0,2,1:T(8,128)S(1)} %get-tuple-element.19, f32[2,256,256,8]{2,1,3,0:T(8,128)S(1)} %copy-done.2, ...), kind=kLoop, calls=%fused_computation.16 | loop fusion | flops 8380416 | bytes 8585216 | tf_op jit(solution)/shard_map/reduce_sum | solution.py:54
  121.4 1.1 fusion.36
  122.6 1.1 fusion.26
  123.7 2.0 %fusion.12 = (f32[256,2,8]{0,2,1:T(8,128)S(1)}, f32[256,2,8]{0,2,1:T(8,128)S(1)}) fusion(f32[2,256,256,8]{2,1,3,0:T(8,128)S(1)} %get-tuple-element.54, f32[256,2,8]{0,2,1:T(8,128)S(1)} %get-tuple-element.14, pred[256,256]{0,1:T(8,128)(4,1)S(1)} %get-tuple-element.48, f32[256,2,8]{0,2,1:T(8,128)S(1)} %get-tuple-element.13, ...), kind=kLoop, calls=%fused_computation.28 | loop fusion | flops 8380416 | bytes 8585216 | tf_op jit(solution)/shard_map/reduce_sum | solution.py:54
  125.8 2.5 %fusion.41 = bf16[256,2,8,128]{0,3,2,1:T(8,128)(2,1)S(1)} fusion(f32[2,128,256,8]{2,1,3,0:T(8,128)S(1)} %fusion.26, f32[2,128,256,8]{2,1,3,0:T(8,128)S(1)} %fusion.28, f32[2,128,256,8]{2,1,3,0:T(8,128)S(1)} %fusion.30, f32[2,128,256,8]{2,1,3,0:T(8,128)S(1)} %fusion.32, f32[2,128,256,8]{2,1,3,0:T(8,128)S(1)} %fusion.34, f32[2,128,256,8]{2,1,3,0:T(8,128)S(1)} %fusion.36, ...), kind=kOutput, calls=%fused_computation.50 | convolution fusion | flops 281542656 | bytes 20283392 | tf_op jit(solution)/shard_map/qcgk,kcd->qcgd/dot_general | solution.py:56
  128.3 1.4 %copy.144 = bf16[256,2048]{1,0:T(8,128)(2,1)} copy(bf16[256,2048]{0,1:T(8,128)(2,1)S(1)} %bitcast.248) | data formatting | bytes 2097152 | tf_op jit(solution)/shard_map/convert_element_type | solution.py:78
  (43 shorter events, 2.2 us)
Async XLA Ops:
  0.0 24.7 %copy-start.13 = (s32[2048]{0:T(1024)S(1)}, s32[2048]{0:T(1024)}, u32[]{:S(2)}) copy-start(s32[2048]{0:T(1024)} %param.7) | copy-start | bytes 24580
  1.6 7.5 %all-to-all-start = ((bf16[64,4,256]{2,0,1:T(8,128)(2,1)}), bf16[64,4,256]{2,0,1:T(8,128)(2,1)S(1)}, u32[]{:S(2)}, u32[]{:S(2)}) async-start(bf16[64,4,256]{2,0,1:T(8,128)(2,1)} %bitcast.233), calls=%async_computation | async-start | bytes 262144 | tf_op jit(solution)/shard_map/all_to_all | solution.py:21
  9.1 7.9 %all-to-all-start.2 = ((bf16[64,4,256]{2,0,1:T(8,128)(2,1)}), bf16[64,4,256]{2,0,1:T(8,128)(2,1)S(1)}, u32[]{:S(2)}, u32[]{:S(2)}) async-start(bf16[64,4,256]{2,0,1:T(8,128)(2,1)} %bitcast.232), calls=%async_computation.2 | async-start | bytes 262144 | tf_op jit(solution)/shard_map/all_to_all | solution.py:22
  17.0 18.8 %all-to-all-start.1 = ((bf16[64,4,2048]{2,0,1:T(8,128)(2,1)}), bf16[64,4,2048]{2,0,1:T(8,128)(2,1)S(1)}, u32[]{:S(2)}, u32[]{:S(2)}) async-start(bf16[64,4,2048]{2,0,1:T(8,128)(2,1)} %bitcast.231), calls=%async_computation.1 | async-start | bytes 2097152 | tf_op jit(solution)/shard_map/all_to_all | solution.py:20
  21.6 10.6 %collective-permute-start = (bf16[1,2,256,256]{3,2,1,0:T(8,128)(2,1)S(1)}, bf16[1,2,256,256]{3,2,1,0:T(8,128)(2,1)S(1)}, u32[]{:S(2)}, u32[]{:S(2)}) collective-permute-start(bf16[1,2,256,256]{3,2,1,0:T(8,128)(2,1)S(1)} %maximum_bitcast_fusion), channel_id=1, source_target_pairs={{0,4},{4,8},{8,12},{12,16},{16,20},{20,24},{24,28},{1,5},{5,9},{9,... | collective-permute-start | bytes 786440 | tf_op jit(solution)/shard_map/ppermute | solution.py:15
  34.5 14.7 %collective-permute-start.1 = (bf16[2,2,256,256]{3,2,1,0:T(8,128)(2,1)}, bf16[2,2,256,256]{3,2,1,0:T(8,128)(2,1)S(1)}, u32[]{:S(2)}, u32[]{:S(2)}) collective-permute-start(bf16[2,2,256,256]{3,2,1,0:T(8,128)(2,1)} %pad_maximum_fusion.1), channel_id=1, source_target_pairs={{0,8},{4,12},{8,16},{12,20},{16,24},{20,28},{1,9},{5,13},{9,17},{1... | collective-permute-start | bytes 1572872 | tf_op jit(solution)/shard_map/ppermute | solution.py:15
  37.9 12.4 %copy-start = (f32[2,256,256,8]{2,1,3,0:T(8,128)}, f32[2,256,256,8]{2,1,3,0:T(8,128)S(1)}, u32[]{:S(2)}) copy-start(f32[2,256,256,8]{2,1,3,0:T(8,128)S(1)} %get-tuple-element.64) | copy-start | bytes 12582916
  37.9 13.9 %copy-start.9 = (bf16[1,1,256,256]{2,3,1,0:T(8,128)(2,1)S(1)}, bf16[1,1,256,256]{2,3,1,0:T(8,128)(2,1)}, u32[]{:S(2)}) copy-start(bf16[1,1,256,256]{2,3,1,0:T(8,128)(2,1)} %copy.109) | copy-start | bytes 393220
  50.3 50.4 %collective-permute-start.2 = (bf16[4,2,256,256]{3,2,1,0:T(8,128)(2,1)}, bf16[4,2,256,256]{3,2,1,0:T(8,128)(2,1)S(1)}, u32[]{:S(2)}, u32[]{:S(2)}) collective-permute-start(bf16[4,2,256,256]{3,2,1,0:T(8,128)(2,1)} %pad_maximum_fusion), channel_id=1, source_target_pairs={{0,16},{4,20},{8,24},{12,28},{1,17},{5,21},{9,25},{13,29},{2,18},{... | collective-permute-start | bytes 3145736 | tf_op jit(solution)/shard_map/ppermute | solution.py:15
  101.5 3.7 %copy-start.6 = (pred[256,256]{0,1:T(8,128)(4,1)S(1)}, pred[256,256]{0,1:T(8,128)(4,1)}, u32[]{:S(2)}) copy-start(pred[256,256]{0,1:T(8,128)(4,1)} %get-tuple-element.47) | copy-start | bytes 196612
  105.2 2.0 %copy-start.7 = (pred[256,256]{0,1:T(8,128)(4,1)S(1)}, pred[256,256]{0,1:T(8,128)(4,1)}, u32[]{:S(2)}) copy-start(pred[256,256]{0,1:T(8,128)(4,1)} %get-tuple-element.49) | copy-start | bytes 196612
  106.2 2.0 %copy-start.10 = (f32[256,2,8]{0,2,1:T(8,128)S(1)}, f32[256,2,8]{0,2,1:T(8,128)}, u32[]{:S(2)}) copy-start(f32[256,2,8]{0,2,1:T(8,128)} %get-tuple-element.65) | copy-start | bytes 49156
  106.2 2.0 %copy-start.11 = (f32[256,2,8]{0,2,1:T(8,128)S(1)}, f32[256,2,8]{0,2,1:T(8,128)}, u32[]{:S(2)}) copy-start(f32[256,2,8]{0,2,1:T(8,128)} %get-tuple-element.61) | copy-start | bytes 49156
  106.2 2.0 %copy-start.12 = (f32[256,2,8]{0,2,1:T(8,128)S(1)}, f32[256,2,8]{0,2,1:T(8,128)}, u32[]{:S(2)}) copy-start(f32[256,2,8]{0,2,1:T(8,128)} %get-tuple-element.59) | copy-start | bytes 49156
  111.4 2.2 %copy-start.4 = (f32[2,256,256,8]{2,1,3,0:T(8,128)S(1)}, f32[2,256,256,8]{2,1,3,0:T(8,128)}, u32[]{:S(2)}) copy-start(f32[2,256,256,8]{2,1,3,0:T(8,128)} %get-tuple-element.60) | copy-start | bytes 12582916
  112.6 2.5 %copy-start.3 = (f32[2,256,256,8]{2,1,3,0:T(8,128)S(1)}, f32[2,256,256,8]{2,1,3,0:T(8,128)}, u32[]{:S(2)}) copy-start(f32[2,256,256,8]{2,1,3,0:T(8,128)} %get-tuple-element.62) | copy-start | bytes 12582916
  115.1 3.2 %copy-start.2 = (f32[2,256,256,8]{2,1,3,0:T(8,128)S(1)}, f32[2,256,256,8]{2,1,3,0:T(8,128)}, u32[]{:S(2)}) copy-start(f32[2,256,256,8]{2,1,3,0:T(8,128)} %get-tuple-element.66) | copy-start | bytes 12582916
  117.2 2.2 %copy-start.1 = (f32[2,256,256,8]{2,1,3,0:T(8,128)S(1)}, f32[2,256,256,8]{2,1,3,0:T(8,128)}, u32[]{:S(2)}) copy-start(f32[2,256,256,8]{2,1,3,0:T(8,128)} %copy-done) | copy-start | bytes 12582916
  119.4 2.0 %copy-start.8 = (bf16[1,1,256,256]{2,3,1,0:T(8,128)(2,1)S(1)}, bf16[1,1,256,256]{2,3,1,0:T(8,128)(2,1)}, u32[]{:S(2)}) copy-start(bf16[1,1,256,256]{2,3,1,0:T(8,128)(2,1)} %copy.112) | copy-start | bytes 393220
  123.7 2.1 %copy-start.5 = (f32[2,256,8,128]{1,3,2,0:T(8,128)S(1)}, f32[2,256,8,128]{1,3,2,0:T(8,128)}, u32[]{:S(2)}) copy-start(f32[2,256,8,128]{1,3,2,0:T(8,128)} %fusion.38) | copy-start | bytes 6291460
where the time goes:
time: 130 us
  waiting for transfers between devices  52.2 us (40%)
  matrix products  29.5 us (23%)
  starting transfers between devices  18.7 us (14%)
  local copies, waits for them, and re-layouts  17.7 us (14%)
  other arithmetic  11.2 us (9%)
    ppermute x3, waiting for transfers between devices, from_behind(): return lax.ppermute(array, axis, pairs)  48.9 us
    dot_general x8, matrix products, absorb(): jnp.einsum('qcgd,kcd->qcgk', query_heads, key_block, preferred_element_ty...  16.3 us
    dot_general x8, matrix products, absorb(): jnp.einsum('qcgk,kcd->qcgd', rounded, value_block, preferred_element_type...  13.2 us
    reduce_sum x4, other arithmetic, absorb(): weight_sum = weight_sum * rescale + jnp.sum(weights, axis=-1)  8.14 us
    ppermute x3, starting transfers between devices, from_behind(): return lax.ppermute(array, axis, pairs)  5.86 us
    slice x10, local copies, waits for them, and re-layouts, absorb(): value_block = key_pair[1].reshape(shard_rows, head_count, HD)  4.61 us
    all_to_all x1, starting transfers between devices, body(): lax.all_to_all(queries, 'head', split_axis=1, concat_axis=0, tiled=True)  4.53 us
    all_to_all x1, starting transfers between devices, body(): lax.all_to_all(values, 'head', split_axis=1, concat_axis=0, tiled=True)  4.33 us
  transfers between devices with their start and end apart: 6, of which 5 were waited for; matrix products, arithmetic and copies ran while one was open for 21% of the time, Pallas kernels for 0%

commit v1 on v0

v1 whole, which is shorter than its diff:
```python
import functools

import jax
import jax.numpy as jnp
from jax import lax
from jax.experimental import pallas as pl
from jax.experimental.pallas import tpu as pltpu
from jax.sharding import PartitionSpec as P

QH = 64
KVH = 8
HD = 128
REACH = 7
GROUPS = QH // KVH
MESH = pl.DeviceIdType.MESH
NEG = -1e30
SCALE = HD ** -0.5 * 1.4426950408889634
ROWS = 128


def kernel(
    tok_len, head_len, hops,
    q_hbm, k_hbm, v_hbm, ids_ref, out_ref,
    q_buf, kv, bias, peak, part, acc,
    own_sem, kv_send, kv_recv, q_send, q_recv, z_send, z_recv, x_send, x_recv,
):
    t, h = lax.axis_index("tok"), lax.axis_index("head")
    level, parity = t // 2, lax.rem(t, 2)
    partner = level * 2 + (1 - parity)
    levels = tok_len // 2
    piece = q_hbm.shape[0]
    kv_heads, shard, wide = q_buf.shape
    q_cols, kv_cols = kv_heads * wide, kv_heads * HD

    barrier = pltpu.get_barrier_semaphore()
    greeted = head_len
    for d in range(1, head_len):
        pl.semaphore_signal(
            barrier, inc=1, device_id={"tok": t, "head": lax.rem(h + d, head_len)}, device_id_type=MESH
        )
    pl.semaphore_signal(barrier, inc=1, device_id={"tok": partner, "head": h}, device_id_type=MESH)
    for k in range(1, hops + 1):
        @pl.when(level + k < levels)
        def _():
            pl.semaphore_signal(barrier, inc=1, device_id={"tok": t + 2 * k, "head": h}, device_id_type=MESH)

        @pl.when(level - k >= 0)
        def _():
            pl.semaphore_signal(barrier, inc=1, device_id={"tok": t - 2 * k, "head": h}, device_id_type=MESH)
    greeted = greeted + jnp.minimum(levels - 1 - level, hops) + jnp.minimum(level, hops)
    pl.semaphore_wait(barrier, greeted)

    rows = pl.ds(pl.multiple_of(h * piece, piece), piece)

    def kv_piece(d, which, source):
        g = lax.rem(h + d, head_len)
        return pltpu.make_async_remote_copy(
            src_ref=source.at[:, pl.ds(pl.multiple_of(g * kv_cols, kv_cols), kv_cols)],
            dst_ref=kv.at[0, parity, which, rows, :],
            send_sem=kv_send.at[d, which],
            recv_sem=kv_recv.at[d, which],
            device_id={"tok": t, "head": g},
            device_id_type=MESH,
        )

    def q_piece(d, c):
        g = lax.rem(h + d, head_len)
        return pltpu.make_async_remote_copy(
            src_ref=q_hbm.at[:, pl.ds(pl.multiple_of(g * q_cols + c * wide, wide), wide)],
            dst_ref=q_buf.at[c, rows, :],
            send_sem=q_send.at[d, c],
            recv_sem=q_recv.at[d, c],
            device_id={"tok": t, "head": g},
            device_id_type=MESH,
        )

    def own_kv(which, source):
        return pltpu.make_async_copy(
            source.at[:, pl.ds(pl.multiple_of(h * kv_cols, kv_cols), kv_cols)],
            kv.at[0, parity, which, rows, :],
            own_sem.at[which],
        )

    def own_q(c):
        return pltpu.make_async_copy(
            q_hbm.at[:, pl.ds(pl.multiple_of(h * q_cols + c * wide, wide), wide)],
            q_buf.at[c, rows, :],
            own_sem.at[2 + c],
        )

    def push(k):
        return pltpu.make_async_remote_copy(
            src_ref=kv.at[0, parity],
            dst_ref=kv.at[k, parity],
            send_sem=z_send.at[k],
            recv_sem=z_recv.at[k],
            device_id={"tok": t + 2 * k, "head": h},
            device_id_type=MESH,
        )

    def share(k):
        return pltpu.make_async_remote_copy(
            src_ref=kv.at[k, parity],
            dst_ref=kv.at[k, parity],
            send_sem=x_send.at[k],
            recv_sem=x_recv.at[k],
            device_id={"tok": partner, "head": h},
            device_id_type=MESH,
        )

    sources = (k_hbm, v_hbm)
    for d in range(1, head_len):
        for which in range(2):
            kv_piece(d, which, sources[which]).start()
    for which in range(2):
        own_kv(which, sources[which]).start()
    for c in range(kv_heads):
        for d in range(1, head_len):
            q_piece(d, c).start()
        own_q(c).start()

    for which in range(2):
        own_kv(which, sources[which]).wait()
        for d in range(1, head_len):
            kv_piece(d, which, sources[which]).wait_recv()
    share(0).start()
    for k in range(1, hops + 1):
        @pl.when(level + k < levels)
        def _():
            push(k).start()

    own_ids = ids_ref[:, pl.ds(pl.multiple_of(t * shard, shard), shard)]
    column = jnp.broadcast_to(own_ids, (2 * shard, shard)).T
    q_pos = t * shard + lax.broadcasted_iota(jnp.int32, (shard, 2 * shard), 0)
    k_iota = lax.broadcasted_iota(jnp.int32, (shard, 2 * shard), 1)
    for k in range(hops + 1):
        @pl.when(level - k >= 0)
        def _():
            start = (level - k) * 2 * shard
            key_ids = ids_ref[:, pl.ds(pl.multiple_of(start, 2 * shard), 2 * shard)]
            visible = (column == key_ids) & (start + k_iota <= q_pos)
            bias[k] = jnp.where(visible, 0.0, NEG)

    def absorb(k, c, first):
        def head(j, carry):
            lanes = pl.ds(pl.multiple_of(j * HD, HD), HD)
            heads = pl.ds(pl.multiple_of(c * HD, HD), HD)
            index = c * GROUPS + j
            keys = [kv[k, s, 0, :, heads] for s in range(2)]
            vals = [kv[k, s, 1, :, heads] for s in range(2)]
            for r in range(0, shard, ROWS):
                q = q_buf[c, pl.ds(r, ROWS), lanes]
                tiles = []
                for s in range(2):
                    score = lax.dot_general(
                        q, keys[s], (((1,), (1,)), ((), ())), preferred_element_type=jnp.float32
                    )
                    score = score * SCALE + bias[k, pl.ds(r, ROWS), s * shard:(s + 1) * shard]
                    tiles += [score[:, i:i + HD] for i in range(0, shard, HD)]
                top = functools.reduce(jnp.maximum, tiles)
                top = jnp.broadcast_to(jnp.max(top, axis=1, keepdims=True), (ROWS, HD))
                if not first:
                    before = peak[index, pl.ds(r, ROWS), :]
                    top = jnp.maximum(before, top)
                    decay = jnp.exp2(before - top)
                peak[index, pl.ds(r, ROWS), :] = top
                weights = [jnp.exp2(tile - top) for tile in tiles]
                total = functools.reduce(jnp.add, weights)
                rounded = [w.astype(jnp.bfloat16) for w in weights]
                half = len(rounded) // 2
                update = jnp.dot(
                    jnp.concatenate(rounded[:half], axis=1), vals[0], preferred_element_type=jnp.float32
                ) + jnp.dot(
                    jnp.concatenate(rounded[half:], axis=1), vals[1], preferred_element_type=jnp.float32
                )
                if not first:
                    total = part[index, pl.ds(r, ROWS), :] * decay + total
                    update = acc[index, pl.ds(r, ROWS), :] * decay + update
                part[index, pl.ds(r, ROWS), :] = total
                acc[index, pl.ds(r, ROWS), :] = update
            return carry

        lax.fori_loop(0, GROUPS, head, 0, unroll=2)

    def relay(k):
        if k <= hops:
            @pl.when(level - k >= 0)
            def _():
                push(k).wait_recv()
                share(k).start()

    relay(1)
    share(0).wait_recv()
    for c in range(kv_heads):
        own_q(c).wait()
        for d in range(1, head_len):
            q_piece(d, c).wait_recv()

        absorb(0, c, True)
    for k in range(1, hops + 1):
        relay(k + 1)

        @pl.when(level - k >= 0)
        def _():
            share(k).wait_recv()

            def pair(c, carry):
                absorb(k, c, False)
                return carry

            lax.fori_loop(0, kv_heads, pair, 0)

    def finish(index, carry):
        total = jnp.sum(part[index], axis=1, keepdims=True)
        result = (acc[index] * (1.0 / total)).astype(out_ref.dtype)
        out_ref[:, pl.ds(pl.multiple_of(index * HD, HD), HD)] = result
        return carry

    lax.fori_loop(0, kv_heads * GROUPS, finish, 0, unroll=2)

    for d in range(1, head_len):
        for which in range(2):
            kv_piece(d, which, sources[which]).wait_send()
        for c in range(kv_heads):
            q_piece(d, c).wait_send()
    share(0).wait_send()
    for k in range(1, hops + 1):
        @pl.when(level + k < levels)
        def _():
            push(k).wait_send()

        @pl.when(level - k >= 0)
        def _():
            share(k).wait_send()


def body(queries, keys, values, doc_ids):
    tok_len, head_len = lax.axis_size("tok"), lax.axis_size("head")
    shard = queries.shape[0] * head_len
    kv_heads = KVH // head_len
    wide = GROUPS * HD
    hops = min((REACH + 1) // 2, tok_len // 2 - 1)
    heads = kv_heads * GROUPS
    DMA = pltpu.SemaphoreType.DMA
    anywhere = pl.BlockSpec(memory_space=pl.ANY)
    vmem = pl.BlockSpec(memory_space=pltpu.VMEM)
    return pl.pallas_call(
        functools.partial(kernel, tok_len, head_len, hops),
        out_shape=jax.ShapeDtypeStruct((shard, heads * HD), jnp.bfloat16),
        in_specs=[anywhere, anywhere, anywhere, vmem],
        out_specs=vmem,
        scratch_shapes=[
            pltpu.VMEM((kv_heads, shard, wide), jnp.bfloat16),
            pltpu.VMEM((hops + 1, 2, 2, shard, kv_heads * HD), jnp.bfloat16),
            pltpu.VMEM((hops + 1, shard, 2 * shard), jnp.float32),
            pltpu.VMEM((heads, shard, HD), jnp.float32),
            pltpu.VMEM((heads, shard, HD), jnp.float32),
            pltpu.VMEM((heads, shard, HD), jnp.float32),
            DMA((2 + kv_heads,)),
            DMA((head_len, 2)),
            DMA((head_len, 2)),
            DMA((head_len, kv_heads)),
            DMA((head_len, kv_heads)),
            DMA((hops + 1,)),
            DMA((hops + 1,)),
            DMA((hops + 1,)),
            DMA((hops + 1,)),
        ],
        compiler_params=pltpu.CompilerParams(
            collective_id=0, has_side_effects=True, vmem_limit_bytes=48 * 1024 * 1024
        ),
    )(queries, keys, values, doc_ids.reshape(1, -1))


def solution(mesh):
    return jax.shard_map(
        body,
        mesh=mesh,
        in_specs=(
            P(("tok", "head"), None),
            P(("tok", "head"), None),
            P(("tok", "head"), None),
            P(),
        ),
        out_specs=P("tok", "head"),
        check_vma=False,
    )
```

time: 130 us -> 67.6 us (0.52)
  Pallas kernels: 0 us -> 62.6 us
  waiting for transfers between devices: 52.2 us -> 0 us
  matrix products: 29.5 us -> 0 us
  starting transfers between devices: 18.7 us -> 0 us
  local copies, waits for them, and re-layouts: 17.7 us -> 4.7 us
  other arithmetic: 11.2 us -> 0 us
    pallas_call x0 -> x1, Pallas kernels: none -> 62.6 us  [body(): pl.pallas_call(functools.partial(kernel, tok_len, head_len, hops), out_sh...]
    ppermute x3 -> x0, waiting for transfers between devices: 48.9 us -> none  [from_behind(): return lax.ppermute(array, axis, pairs)]
    dot_general x16 -> x0, matrix products: 29.5 us -> none  [the longest x8 16.3 us: absorb(): jnp.einsum('qcgd,kcd->qcgk', query_heads, key_block, preferred_element_ty...]
    all_to_all x3 -> x0, starting transfers between devices: 12.8 us -> none  [the longest x1 4.53 us: body(): lax.all_to_all(queries, 'head', split_axis=1, concat_axis=0, tiled=True)]
    reduce_sum x4 -> x0, other arithmetic: 8.14 us -> none  [absorb(): weight_sum = weight_sum * rescale + jnp.sum(weights, axis=-1)]
    slice x17 -> x0, local copies, waits for them, and re-layouts: 6.87 us -> none  [the longest x10 4.61 us: absorb(): value_block = key_pair[1].reshape(shard_rows, head_count, HD)]
    ppermute x3 -> x0, starting transfers between devices: 5.86 us -> none  [from_behind(): return lax.ppermute(array, axis, pairs)]
    all_to_all x3 -> x0, local copies, waits for them, and re-layouts: 5.43 us -> none  [the longest x1 2.3 us: body(): lax.all_to_all(queries, 'head', split_axis=1, concat_axis=0, tiled=True)]
  transfers between devices with their start and end apart: 6 -> 0, of which waited for: 5 -> 0; matrix products, arithmetic and copies ran while one was open for 21% -> 0% of each run, Pallas kernels for 0% -> 0%
where the time goes in v1:
time: 67.6 us; the launch traced here: 67.4 us
  Pallas kernels  62.6 us (93%)
  local copies, waits for them, and re-layouts  4.7 us (7%)
    pallas_call x1, Pallas kernels, body(): pl.pallas_call(functools.partial(kernel, tok_len, head_len, hops), out_sh...  62.6 us
    unnamed x9, local copies, waits for them, and re-layouts  4.7 us

profile of v1, /device:TPU:25, one launch (start us, length us, event | category | flops | bytes accessed | tf_op | source)
XLA Modules:
  0.0 67.4 jit_solution(1535946420991511283)
XLA Ops:
  0.0 0.0 copy-start
  0.0 1.2 %copy-done = bf16[64,8192]{1,0:T(8,128)(2,1)S(1)} copy-done((bf16[64,8192]{1,0:T(8,128)(2,1)S(1)}, bf16[64,8192]{1,0:T(8,128)(2,1)}, u32[]{:S(2)}) %copy-start) | copy-done | bytes 1048600
  1.2 0.0 copy-start.1
  1.2 0.9 %copy-done.1 = bf16[64,1024]{1,0:T(8,128)(2,1)S(1)} copy-done((bf16[64,1024]{1,0:T(8,128)(2,1)S(1)}, bf16[64,1024]{1,0:T(8,128)(2,1)}, u32[]{:S(2)}) %copy-start.1) | copy-done | bytes 131096
  2.1 0.0 copy-start.2
  2.1 0.9 %copy-done.2 = bf16[64,1024]{1,0:T(8,128)(2,1)S(1)} copy-done((bf16[64,1024]{1,0:T(8,128)(2,1)S(1)}, bf16[64,1024]{1,0:T(8,128)(2,1)}, u32[]{:S(2)}) %copy-start.2) | copy-done | bytes 131096
  3.0 0.0 copy-start.3
  3.0 0.7 %copy-done.3 = s32[2048]{0:T(1024)S(1)} copy-done((s32[2048]{0:T(1024)S(1)}, s32[2048]{0:T(1024)}, u32[]{:S(2)}) %copy-start.3) | copy-done | bytes 8216
  3.7 62.6 %shard_map.46 = bf16[256,2048]{1,0:T(8,128)(2,1)S(1)} custom-call(bf16[64,8192]{1,0:T(8,128)(2,1)S(1)} %copy-done, bf16[64,1024]{1,0:T(8,128)(2,1)S(1)} %copy-done.1, bf16[64,1024]{1,0:T(8,128)(2,1)S(1)} %copy-done.2, s32[1,2048]{1,0:T(1,128)S(1)} %bitcast.1), custom_call_target="tpu_custom_call" | custom-call | tf_op jit(solution)/shard_map/pallas_call | solution.py:247
  66.4 1.0 %copy.6 = bf16[256,2048]{1,0:T(8,128)(2,1)} copy(bf16[256,2048]{1,0:T(8,128)(2,1)S(1)} %shard_map.46) | data formatting | bytes 2097152
Async XLA Ops:
  0.0 1.2 %copy-start = (bf16[64,8192]{1,0:T(8,128)(2,1)S(1)}, bf16[64,8192]{1,0:T(8,128)(2,1)}, u32[]{:S(2)}) copy-start(bf16[64,8192]{1,0:T(8,128)(2,1)} %q_hbm.1) | copy-start | bytes 3145732
  1.2 0.9 %copy-start.1 = (bf16[64,1024]{1,0:T(8,128)(2,1)S(1)}, bf16[64,1024]{1,0:T(8,128)(2,1)}, u32[]{:S(2)}) copy-start(bf16[64,1024]{1,0:T(8,128)(2,1)} %k_hbm.1) | copy-start | bytes 393220
  2.1 0.9 %copy-start.2 = (bf16[64,1024]{1,0:T(8,128)(2,1)S(1)}, bf16[64,1024]{1,0:T(8,128)(2,1)}, u32[]{:S(2)}) copy-start(bf16[64,1024]{1,0:T(8,128)(2,1)} %v_hbm.1) | copy-start | bytes 393220
  3.0 0.7 %copy-start.3 = (s32[2048]{0:T(1024)S(1)}, s32[2048]{0:T(1024)}, u32[]{:S(2)}) copy-start(s32[2048]{0:T(1024)} %param.7) | copy-start | bytes 24580

commit v2 on v1

--- a/solution.py
+++ b/solution.py
@@ -15,7 +15,7 @@
 MESH = pl.DeviceIdType.MESH
 NEG = -1e30
 SCALE = HD ** -0.5 * 1.4426950408889634
-ROWS = 128
+ROWS = 256
 
 
 def kernel(
@@ -88,22 +88,22 @@
             own_sem.at[2 + c],
         )
 
-    def push(k):
+    def push(k, which):
         return pltpu.make_async_remote_copy(
-            src_ref=kv.at[0, parity],
-            dst_ref=kv.at[k, parity],
-            send_sem=z_send.at[k],
-            recv_sem=z_recv.at[k],
+            src_ref=kv.at[0, parity, which],
+            dst_ref=kv.at[k, parity, which],
+            send_sem=z_send.at[k, which],
+            recv_sem=z_recv.at[k, which],
             device_id={"tok": t + 2 * k, "head": h},
             device_id_type=MESH,
         )
 
-    def share(k):
+    def share(k, which):
         return pltpu.make_async_remote_copy(
-            src_ref=kv.at[k, parity],
-            dst_ref=kv.at[k, parity],
-            send_sem=x_send.at[k],
-            recv_sem=x_recv.at[k],
+            src_ref=kv.at[k, parity, which],
+            dst_ref=kv.at[k, parity, which],
+            send_sem=x_send.at[k, which],
+            recv_sem=x_recv.at[k, which],
             device_id={"tok": partner, "head": h},
             device_id_type=MESH,
         )
@@ -114,20 +114,24 @@
             kv_piece(d, which, sources[which]).start()
     for which in range(2):
         own_kv(which, sources[which]).start()
+    for which in range(2):
+        own_kv(which, sources[which]).wait()
+        for d in range(1, head_len):
+            kv_piece(d, which, sources[which]).wait_recv()
+        share(0, which).start()
+        for k in range(1, 2):
+            @pl.when(level + k < levels)
+            def _():
+                push(k, which).start()
+    for k in range(2, hops + 1):
+        @pl.when(level + k < levels)
+        def _():
+            for which in range(2):
+                push(k, which).start()
     for c in range(kv_heads):
         for d in range(1, head_len):
             q_piece(d, c).start()
         own_q(c).start()
-
-    for which in range(2):
-        own_kv(which, sources[which]).wait()
-        for d in range(1, head_len):
-            kv_piece(d, which, sources[which]).wait_recv()
-    share(0).start()
-    for k in range(1, hops + 1):
-        @pl.when(level + k < levels)
-        def _():
-            push(k).start()
 
     own_ids = ids_ref[:, pl.ds(pl.multiple_of(t * shard, shard), shard)]
     column = jnp.broadcast_to(own_ids, (2 * shard, shard)).T
@@ -141,43 +145,44 @@
             visible = (column == key_ids) & (start + k_iota <= q_pos)
             bias[k] = jnp.where(visible, 0.0, NEG)
 
-    def absorb(k, c, first):
+    def absorb(k, c, shards, first):
         def head(j, carry):
             lanes = pl.ds(pl.multiple_of(j * HD, HD), HD)
             heads = pl.ds(pl.multiple_of(c * HD, HD), HD)
             index = c * GROUPS + j
-            keys = [kv[k, s, 0, :, heads] for s in range(2)]
-            vals = [kv[k, s, 1, :, heads] for s in range(2)]
-            for r in range(0, shard, ROWS):
-                q = q_buf[c, pl.ds(r, ROWS), lanes]
-                tiles = []
-                for s in range(2):
-                    score = lax.dot_general(
-                        q, keys[s], (((1,), (1,)), ((), ())), preferred_element_type=jnp.float32
-                    )
-                    score = score * SCALE + bias[k, pl.ds(r, ROWS), s * shard:(s + 1) * shard]
-                    tiles += [score[:, i:i + HD] for i in range(0, shard, HD)]
-                top = functools.reduce(jnp.maximum, tiles)
-                top = jnp.broadcast_to(jnp.max(top, axis=1, keepdims=True), (ROWS, HD))
-                if not first:
-                    before = peak[index, pl.ds(r, ROWS), :]
-                    top = jnp.maximum(before, top)
-                    decay = jnp.exp2(before - top)
-                peak[index, pl.ds(r, ROWS), :] = top
-                weights = [jnp.exp2(tile - top) for tile in tiles]
-                total = functools.reduce(jnp.add, weights)
-                rounded = [w.astype(jnp.bfloat16) for w in weights]
-                half = len(rounded) // 2
-                update = jnp.dot(
-                    jnp.concatenate(rounded[:half], axis=1), vals[0], preferred_element_type=jnp.float32
-                ) + jnp.dot(
-                    jnp.concatenate(rounded[half:], axis=1), vals[1], preferred_element_type=jnp.float32
+            keys = [kv[k, s, 0, :, heads] for s in shards]
+            vals = [kv[k, s, 1, :, heads] for s in shards]
+            q = q_buf[c, :, lanes]
+            tiles = []
+            for s, key in zip(shards, keys):
+                score = lax.dot_general(
+                    q, key, (((1,), (1,)), ((), ())), preferred_element_type=jnp.float32
                 )
-                if not first:
-                    total = part[index, pl.ds(r, ROWS), :] * decay + total
-                    update = acc[index, pl.ds(r, ROWS), :] * decay + update
-                part[index, pl.ds(r, ROWS), :] = total
-                acc[index, pl.ds(r, ROWS), :] = update
+                score = score * SCALE + bias[k, :, pl.ds(pl.multiple_of(s * shard, shard), shard)]
+                tiles += [score[:, i:i + HD] for i in range(0, shard, HD)]
+            top = functools.reduce(jnp.maximum, tiles)
+            top = jnp.broadcast_to(jnp.max(top, axis=1, keepdims=True), (shard, HD))
+            if not first:
+                before = peak[index]
+                top = jnp.maximum(before, top)
+                decay = jnp.exp2(before - top)
+            peak[index] = top
+            weights = [jnp.exp2(tile - top) for tile in tiles]
+            total = functools.reduce(jnp.add, weights)
+            rounded = [w.astype(jnp.bfloat16) for w in weights]
+            step = shard // HD
+            update = functools.reduce(jnp.add, [
+                jnp.dot(
+                    jnp.concatenate(rounded[n * step:(n + 1) * step], axis=1), val,
+                    preferred_element_type=jnp.float32,
+                )
+                for n, val in enumerate(vals)
+            ])
+            if not first:
+                total = part[index] * decay + total
+                update = acc[index] * decay + update
+            part[index] = total
+            acc[index] = update
             return carry
 
         lax.fori_loop(0, GROUPS, head, 0, unroll=2)
@@ -186,29 +191,43 @@
         if k <= hops:
             @pl.when(level - k >= 0)
             def _():
-                push(k).wait_recv()
-                share(k).start()
+                for which in range(2):
+                    push(k, which).wait_recv()
+                    share(k, which).start()
+
+    def await_share(k):
+        for which in range(2):
+            share(k, which).wait_recv()
 
     relay(1)
-    share(0).wait_recv()
+    await_share(0)
     for c in range(kv_heads):
         own_q(c).wait()
         for d in range(1, head_len):
             q_piece(d, c).wait_recv()
-
-        absorb(0, c, True)
+        if c == kv_heads - 1:
+            relay(2)
+        absorb(0, c, (0, 1), True)
     for k in range(1, hops + 1):
-        relay(k + 1)
-
         @pl.when(level - k >= 0)
         def _():
-            share(k).wait_recv()
-
-            def pair(c, carry):
-                absorb(k, c, False)
-                return carry
-
-            lax.fori_loop(0, kv_heads, pair, 0)
+            def pair(shards):
+                def run(c, carry):
+                    absorb(k, c, shards, False)
+                    return carry
+
+                lax.fori_loop(0, kv_heads, run, 0)
+
+            if k < hops:
+                await_share(k)
+                for c in range(kv_heads):
+                    if c == kv_heads - 1 and k >= 1:
+                        relay(k + 2)
+                    absorb(k, c, (0, 1), False)
+            else:
+                pair((parity,))
+                await_share(k)
+                pair((1 - parity,))
 
     def finish(index, carry):
         total = jnp.sum(part[index], axis=1, keepdims=True)
@@ -223,15 +242,16 @@
             kv_piece(d, which, sources[which]).wait_send()
         for c in range(kv_heads):
             q_piece(d, c).wait_send()
-    share(0).wait_send()
-    for k in range(1, hops + 1):
-        @pl.when(level + k < levels)
-        def _():
-            push(k).wait_send()
-
-        @pl.when(level - k >= 0)
-        def _():
-            share(k).wait_send()
+    for which in range(2):
+        share(0, which).wait_send()
+        for k in range(1, hops + 1):
+            @pl.when(level + k < levels)
+            def _():
+                push(k, which).wait_send()
+
+            @pl.when(level - k >= 0)
+            def _():
+                share(k, which).wait_send()
 
 
 def body(queries, keys, values, doc_ids):
@@ -261,13 +281,13 @@
             DMA((head_len, 2)),
             DMA((head_len, kv_heads)),
             DMA((head_len, kv_heads)),
-            DMA((hops + 1,)),
-            DMA((hops + 1,)),
-            DMA((hops + 1,)),
-            DMA((hops + 1,)),
+            DMA((hops + 1, 2)),
+            DMA((hops + 1, 2)),
+            DMA((hops + 1, 2)),
+            DMA((hops + 1, 2)),
         ],
         compiler_params=pltpu.CompilerParams(
-            collective_id=0, has_side_effects=True, vmem_limit_bytes=48 * 1024 * 1024
+            collective_id=0, has_side_effects=True, vmem_limit_bytes=64 * 1000 * 1000
         ),
     )(queries, keys, values, doc_ids.reshape(1, -1))
 

time: 67.6 us -> 63.9 us (0.945)
  local copies, waits for them, and re-layouts: 4.7 us -> 2.3 us
  Pallas kernels: 62.6 us -> 61.3 us
    unnamed x9 -> x1, local copies, waits for them, and re-layouts: 4.7 us -> 2.3 us
    pallas_call x1, Pallas kernels: 62.6 us -> 61.3 us  [body(): pl.pallas_call(functools.partial(kernel, tok_len, head_len, hops), out_sh...]
where the time goes in v2:
time: 63.9 us; the launch traced here: 63.6 us
  Pallas kernels  61.3 us (96%)
  local copies, waits for them, and re-layouts  2.3 us (4%)
    pallas_call x1, Pallas kernels, body(): pl.pallas_call(functools.partial(kernel, tok_len, head_len, hops), out_sh...  61.3 us
    unnamed x1, local copies, waits for them, and re-layouts  2.3 us

profile of v2, /device:TPU:25, one launch (start us, length us, event | category | flops | bytes accessed | tf_op | source)
XLA Modules:
  0.0 63.6 jit_solution(17279211094782424524)
XLA Ops:
  0.0 61.3 %shard_map.46 = bf16[256,2048]{1,0:T(8,128)(2,1)} custom-call(bf16[64,8192]{1,0:T(8,128)(2,1)} %q_hbm.1, bf16[64,1024]{1,0:T(8,128)(2,1)} %k_hbm.1, bf16[64,1024]{1,0:T(8,128)(2,1)} %v_hbm.1, s32[1,2048]{1,0:T(1,128)} %bitcast.1), custom_call_target="tpu_custom_call" | custom-call | tf_op jit(solution)/shard_map/pallas_call | solution.py:267
  61.3 2.3 %copy.6 = bf16[256,2048]{1,0:T(8,128)(2,1)} copy(bf16[256,2048]{1,0:T(8,128)(2,1)} %shard_map.46) | data formatting | bytes 2097152

commit v3 on v2

--- a/solution.py
+++ b/solution.py
@@ -15,7 +15,7 @@
 MESH = pl.DeviceIdType.MESH
 NEG = -1e30
 SCALE = HD ** -0.5 * 1.4426950408889634
-ROWS = 256
+PAIR = 8
 
 
 def kernel(
@@ -146,46 +146,47 @@
             bias[k] = jnp.where(visible, 0.0, NEG)
 
     def absorb(k, c, shards, first):
-        def head(j, carry):
-            lanes = pl.ds(pl.multiple_of(j * HD, HD), HD)
-            heads = pl.ds(pl.multiple_of(c * HD, HD), HD)
-            index = c * GROUPS + j
-            keys = [kv[k, s, 0, :, heads] for s in shards]
-            vals = [kv[k, s, 1, :, heads] for s in shards]
-            q = q_buf[c, :, lanes]
-            tiles = []
-            for s, key in zip(shards, keys):
-                score = lax.dot_general(
-                    q, key, (((1,), (1,)), ((), ())), preferred_element_type=jnp.float32
-                )
-                score = score * SCALE + bias[k, :, pl.ds(pl.multiple_of(s * shard, shard), shard)]
-                tiles += [score[:, i:i + HD] for i in range(0, shard, HD)]
-            top = functools.reduce(jnp.maximum, tiles)
-            top = jnp.broadcast_to(jnp.max(top, axis=1, keepdims=True), (shard, HD))
-            if not first:
-                before = peak[index]
-                top = jnp.maximum(before, top)
-                decay = jnp.exp2(before - top)
-            peak[index] = top
-            weights = [jnp.exp2(tile - top) for tile in tiles]
-            total = functools.reduce(jnp.add, weights)
-            rounded = [w.astype(jnp.bfloat16) for w in weights]
-            step = shard // HD
-            update = functools.reduce(jnp.add, [
-                jnp.dot(
-                    jnp.concatenate(rounded[n * step:(n + 1) * step], axis=1), val,
-                    preferred_element_type=jnp.float32,
-                )
-                for n, val in enumerate(vals)
-            ])
-            if not first:
-                total = part[index] * decay + total
-                update = acc[index] * decay + update
-            part[index] = total
-            acc[index] = update
+        heads = pl.ds(pl.multiple_of(c * HD, HD), HD)
+
+        def stack(j, carry):
+            index = c * GROUPS + j * PAIR
+            keys = jnp.concatenate([kv[k, s, 0, :, heads] for s in shards], axis=0)
+            vals = jnp.concatenate([kv[k, s, 1, :, heads] for s in shards], axis=0)
+            q = jnp.concatenate([
+                q_buf[c, :, pl.ds(pl.multiple_of((j * PAIR + i) * HD, HD), HD)] for i in range(PAIR)
+            ], axis=0)
+            scores = lax.dot_general(
+                q, keys, (((1,), (1,)), ((), ())), preferred_element_type=jnp.float32
+            )
+            rounded, decays = [], []
+            for i in range(PAIR):
+                tiles = []
+                for n, s in enumerate(shards):
+                    part_scores = scores[i * shard:(i + 1) * shard, n * shard:(n + 1) * shard]
+                    part_scores = part_scores * SCALE + bias[k, :, pl.ds(pl.multiple_of(s * shard, shard), shard)]
+                    tiles += [part_scores[:, x:x + HD] for x in range(0, shard, HD)]
+                top = functools.reduce(jnp.maximum, tiles)
+                top = jnp.broadcast_to(jnp.max(top, axis=1, keepdims=True), (shard, HD))
+                if not first:
+                    before = peak[index + i]
+                    top = jnp.maximum(before, top)
+                    decays.append(jnp.exp2(before - top))
+                peak[index + i] = top
+                weights = [jnp.exp2(tile - top) for tile in tiles]
+                total = functools.reduce(jnp.add, weights)
+                if not first:
+                    total = part[index + i] * decays[i] + total
+                part[index + i] = total
+                rounded.append(jnp.concatenate([w.astype(jnp.bfloat16) for w in weights], axis=1))
+            update = jnp.dot(jnp.concatenate(rounded, axis=0), vals, preferred_element_type=jnp.float32)
+            for i in range(PAIR):
+                mine = update[i * shard:(i + 1) * shard]
+                if not first:
+                    mine = acc[index + i] * decays[i] + mine
+                acc[index + i] = mine
             return carry
 
-        lax.fori_loop(0, GROUPS, head, 0, unroll=2)
+        lax.fori_loop(0, GROUPS // PAIR, stack, 0)
 
     def relay(k):
         if k <= hops:

time: 63.9 us -> 50.6 us (0.79)
  Pallas kernels: 61.3 us -> 47.5 us
    pallas_call x1, Pallas kernels: 61.3 us -> 47.5 us  [body(): pl.pallas_call(functools.partial(kernel, tok_len, head_len, hops), out_sh...]
where the time goes in v3:
time: 50.6 us; the launch traced here: 49.9 us
  Pallas kernels  47.5 us (94%)
  local copies, waits for them, and re-layouts  2.3 us (5%)
    pallas_call x1, Pallas kernels, body(): pl.pallas_call(functools.partial(kernel, tok_len, head_len, hops), out_sh...  47.5 us
    unnamed x1, local copies, waits for them, and re-layouts  2.3 us

profile of v3, /device:TPU:25, one launch (start us, length us, event | category | flops | bytes accessed | tf_op | source)
XLA Modules:
  0.0 49.9 jit_solution(11562319236517663655)
XLA Ops:
  0.0 47.5 %shard_map.46 = bf16[256,2048]{1,0:T(8,128)(2,1)} custom-call(bf16[64,8192]{1,0:T(8,128)(2,1)} %q_hbm.1, bf16[64,1024]{1,0:T(8,128)(2,1)} %k_hbm.1, bf16[64,1024]{1,0:T(8,128)(2,1)} %v_hbm.1, s32[1,2048]{1,0:T(1,128)} %bitcast.1), custom_call_target="tpu_custom_call" | custom-call | tf_op jit(solution)/shard_map/pallas_call | solution.py:268
  47.6 2.3 %copy.6 = bf16[256,2048]{1,0:T(8,128)(2,1)} copy(bf16[256,2048]{1,0:T(8,128)(2,1)} %shard_map.46) | data formatting | bytes 2097152
